TPU v7x, 32 devices: a whole 2x2x4 slice. The times are simulated.
32 devices in a mesh: gx: 4 (over y, core), gy: 8 (over z, x).
Axes of the slice: x: 2, y: 2, z: 4, core: 2. Of those that a mesh axis runs over, the one named last changes fastest.
Arguments:
- velocity: float32 [3, 32, 64, 128], P(None, 'gx', 'gy'), may hold values from -6 to 6
- viscosity: float32 [32, 64, 128], P('gx', 'gy'), may hold values from 0.02 to 0.16
- forcing: float32 [4, 3, 32, 64, 128], P(None, None, 'gx', 'gy'), may hold values from -6 to 6
- earlier: float32 [60, 3, 32, 64, 128], P(None, None, 'gx', 'gy'), may hold values from -12 to 12
Outputs:
- velocity_out: float32 [3, 32, 64, 128], P(None, 'gx', 'gy')
- basis: float32 [64, 3, 32, 64, 128], P(None, None, 'gx', 'gy')
- factor: float32 [64, 64], replicated
All inputs are finite; a program needn't handle non-finite values.
Results may differ from a plain program's by a relative error of at most 0.000068.
Values sent between devices are 32-bit elements; how exact they have to be, the bound alone decides.
No kernel may reach another device: no remote copies, remote signals or barrier semaphores. Data moves between devices by JAX's collectives and lax.ppermute only.
A program may use at most 64 MiB of HBM per device.

v0:
```python
import jax
import jax.numpy as jnp
from jax import lax
from jax.sharding import PartitionSpec as P


def padded_2(array, sides, width):
    for axis, dim in sides:
        count, length = (lax.axis_size(axis), array.shape[dim])
        up = [(i, (i + 1) % count) for i in range(count - 1)]
        down = [(j, i) for i, j in up]
        last = lax.slice_in_dim(array, length - width, length, axis=dim)
        initial = lax.slice_in_dim(array, 0, width, axis=dim)
        before = lax.ppermute(last, axis, up)
        after = lax.ppermute(initial, axis, down)
        array = jnp.concatenate([before, array, after], axis=dim)
    return array


def laplace(padded, visc_pad):
    size_x = padded.shape[1] - 2
    size_y = padded.shape[2] - 2
    size_z = padded.shape[3] - 2
    centre = padded[:, 1 : 1 + size_x, 1 : 1 + size_y, 1 : 1 + size_z]
    visc_mid = visc_pad[1 : 1 + size_x, 1 : 1 + size_y, 1 : 1 + size_z]
    result = jnp.zeros_like(centre)
    for offset in ((2, 1, 1), (0, 1, 1), (1, 2, 1), (1, 0, 1), (1, 1, 2), (1, 1, 0)):
        first, second, third = offset
        beside = padded[:, first : first + size_x, second : second + size_y, third : third + size_z]
        visc_beside = visc_pad[
            first : first + size_x, second : second + size_y, third : third + size_z
        ]
        result = result + 0.5 * (visc_mid + visc_beside) * (beside - centre)
    return result


def factorize(panel, total_rows):
    local_gram = (
        lax.dot_general(
            panel,
            panel,
            (((1,), (1,)), ((), ())),
            precision=lax.Precision.HIGHEST,
            preferred_element_type=jnp.float32,
        )
        / total_rows
    )
    lower_factor = jnp.linalg.cholesky(lax.psum(local_gram, ("gx", "gy")))
    basis = jax.scipy.linalg.solve_triangular(lower_factor, panel, lower=True)
    return (lower_factor, basis)


def fields_rim_each(velocity, viscosity, forcing):
    visc_halo = padded_2(viscosity, (("gx", 0), ("gy", 1)), 1)
    visc_pad = jnp.pad(visc_halo, ((0, 0), (0, 0), (1, 1)))
    field = velocity
    fields = []
    for index in range(forcing.shape[0]):
        field_halo = padded_2(field, (("gx", 1), ("gy", 2)), 1)
        padded = jnp.pad(field_halo, ((0, 0), (0, 0), (0, 0), (1, 1)))
        field = field + laplace(padded, visc_pad) + forcing[index]
        fields.append(field)
    return fields


def local(velocity, viscosity, forcing, earlier):
    cell_rows = velocity.shape[0] * velocity.shape[1] * velocity.shape[2] * velocity.shape[3]
    total_rows = cell_rows * lax.axis_size("gx") * lax.axis_size("gy")
    fields = fields_rim_each(velocity, viscosity, forcing)
    panel_old = earlier.reshape(earlier.shape[0], cell_rows)
    snapshots = [field.reshape(1, cell_rows) for field in fields]
    lower_factor, basis = factorize(jnp.concatenate([panel_old] + snapshots, 0), total_rows)
    return (fields[-1], basis.reshape((basis.shape[0],) + velocity.shape), lower_factor.T)


def solution(mesh):
    return jax.shard_map(
        local,
        mesh=mesh,
        in_specs=(
            P(None, "gx", "gy", None),
            P("gx", "gy", None),
            P(None, None, "gx", "gy", None),
            P(None, None, "gx", "gy", None),
        ),
        out_specs=(P(None, "gx", "gy", None), P(None, None, "gx", "gy", None), P()),
        check_vma=False,
    )
```

profile of v0, /device:TPU:0, one launch (start us, length us, event | category | flops | bytes accessed | tf_op | source)
XLA Modules:
  0.0 195.6 jit_solution(2520877468651563737)
XLA Ops:
  1.5 2.6 %collective-permute-start.2 = (f32[1,8,128]{2,1,0:T(8,128)S(1)}, f32[1,8,128]{2,1,0:T(8,128)S(1)}, u32[]{:S(2)}, u32[]{:S(2)}) collective-permute-start(f32[1,8,128]{2,1,0:T(8,128)S(1)} %get-tuple-element.39), channel_id=1, source_target_pairs={{0,8},{8,16},{16,24},{1,9},{9,17},{17,25},{2,10},{10,18},{18,26},{... | collective-permute-start | bytes 12296 | tf_op jit(solution)/shard_map/ppermute | solution.py:14
  5.4 3.9 %collective-permute-done = f32[1,8,128]{2,1,0:T(8,128)S(1)} collective-permute-done((f32[1,8,128]{2,1,0:T(8,128)S(1)}, f32[1,8,128]{2,1,0:T(8,128)S(1)}, u32[]{:S(2)}, u32[]{:S(2)}) %collective-permute-start) | collective-permute-done | bytes 4128 | tf_op jit(solution)/shard_map/ppermute | solution.py:15
  10.2 3.4 %collective-permute-start.6 = (f32[10,1,128]{2,1,0:T(1,128)S(1)}, f32[10,1,128]{2,1,0:T(1,128)S(1)}, u32[]{:S(2)}, u32[]{:S(2)}) collective-permute-start(f32[10,1,128]{2,1,0:T(1,128)S(1)} %get-tuple-element.29), channel_id=1, source_target_pairs={{0,1},{1,2},{2,3},{3,4},{4,5},{5,6},{6,7},{8,9},{9,10},{10,11},{11... | collective-permute-start | bytes 15368 | tf_op jit(solution)/shard_map/ppermute | solution.py:14
  16.9 4.6 %collective-permute-start.3 = (f32[3,1,8,128]{3,2,1,0:T(8,128)S(1)}, f32[3,1,8,128]{3,2,1,0:T(8,128)S(1)}, u32[]{:S(2)}, u32[]{:S(2)}) collective-permute-start(f32[3,1,8,128]{3,2,1,0:T(8,128)S(1)} %get-tuple-element.26), channel_id=1, source_target_pairs={{0,8},{8,16},{16,24},{1,9},{9,17},{17,25},{2,10},{10,18},{18,26},{... | collective-permute-start | bytes 36872 | tf_op jit(solution)/shard_map/ppermute | solution.py:14
  23.3 4.3 %collective-permute-start.7 = (f32[3,10,1,128]{3,2,1,0:T(1,128)S(1)}, f32[3,10,1,128]{3,2,1,0:T(1,128)S(1)}, u32[]{:S(2)}, u32[]{:S(2)}) collective-permute-start(f32[3,10,1,128]{3,2,1,0:T(1,128)S(1)} %get-tuple-element.17), channel_id=1, source_target_pairs={{0,1},{1,2},{2,3},{3,4},{4,5},{5,6},{6,7},{8,9},{9,10},{10,11},{11... | collective-permute-start | bytes 46088 | tf_op jit(solution)/shard_map/ppermute | solution.py:14
  29.8 3.9 %collective-permute-done.5 = f32[3,10,1,128]{3,2,1,0:T(1,128)S(1)} collective-permute-done((f32[3,10,1,128]{3,2,1,0:T(1,128)S(1)}, f32[3,10,1,128]{3,2,1,0:T(1,128)S(1)}, u32[]{:S(2)}, u32[]{:S(2)}) %collective-permute-start.5) | collective-permute-done | bytes 15392 | tf_op jit(solution)/shard_map/ppermute | solution.py:15
  39.0 4.7 %collective-permute-done.8 = f32[3,1,8,128]{3,2,1,0:T(8,128)S(1)} collective-permute-done((f32[3,1,8,128]{3,2,1,0:T(8,128)S(1)}, f32[3,1,8,128]{3,2,1,0:T(8,128)S(1)}, u32[]{:S(2)}, u32[]{:S(2)}) %collective-permute-start.8) | collective-permute-done | bytes 12320 | tf_op jit(solution)/shard_map/ppermute | solution.py:15
  43.7 4.8 %collective-permute-start.11 = (f32[3,10,1,128]{3,2,1,0:T(1,128)S(1)}, f32[3,10,1,128]{3,2,1,0:T(1,128)S(1)}, u32[]{:S(2)}, u32[]{:S(2)}) collective-permute-start(f32[3,10,1,128]{3,2,1,0:T(1,128)S(1)} %get-tuple-element.15), channel_id=1, source_target_pairs={{0,1},{1,2},{2,3},{3,4},{4,5},{5,6},{6,7},{8,9},{9,10},{10,11},{11... | collective-permute-start | bytes 46088 | tf_op jit(solution)/shard_map/ppermute | solution.py:14
  50.0 4.2 %collective-permute-done.10 = f32[3,10,1,128]{3,2,1,0:T(1,128)S(1)} collective-permute-done((f32[3,10,1,128]{3,2,1,0:T(1,128)S(1)}, f32[3,10,1,128]{3,2,1,0:T(1,128)S(1)}, u32[]{:S(2)}, u32[]{:S(2)}) %collective-permute-start.10) | collective-permute-done | bytes 15392 | tf_op jit(solution)/shard_map/ppermute | solution.py:15
  55.6 2.9 %collective-permute-start.13 = (f32[3,1,8,128]{3,2,1,0:T(8,128)S(1)}, f32[3,1,8,128]{3,2,1,0:T(8,128)S(1)}, u32[]{:S(2)}, u32[]{:S(2)}) collective-permute-start(f32[3,1,8,128]{3,2,1,0:T(8,128)S(1)} %get-tuple-element.21), channel_id=1, source_target_pairs={{0,8},{8,16},{16,24},{1,9},{9,17},{17,25},{2,10},{10,18},{18,26},{... | collective-permute-start | bytes 36872 | tf_op jit(solution)/shard_map/ppermute | solution.py:14
  59.8 2.7 %collective-permute-done.12 = f32[3,1,8,128]{3,2,1,0:T(8,128)S(1)} collective-permute-done((f32[3,1,8,128]{3,2,1,0:T(8,128)S(1)}, f32[3,1,8,128]{3,2,1,0:T(8,128)S(1)}, u32[]{:S(2)}, u32[]{:S(2)}) %collective-permute-start.12) | collective-permute-done | bytes 12320 | tf_op jit(solution)/shard_map/ppermute | solution.py:15
  62.5 2.9 %collective-permute-start.15 = (f32[3,10,1,128]{3,2,1,0:T(1,128)S(1)}, f32[3,10,1,128]{3,2,1,0:T(1,128)S(1)}, u32[]{:S(2)}, u32[]{:S(2)}) collective-permute-start(f32[3,10,1,128]{3,2,1,0:T(1,128)S(1)} %get-tuple-element.13), channel_id=1, source_target_pairs={{0,1},{1,2},{2,3},{3,4},{4,5},{5,6},{6,7},{8,9},{9,10},{10,11},{11... | collective-permute-start | bytes 46088 | tf_op jit(solution)/shard_map/ppermute | solution.py:14
  66.9 4.2 %collective-permute-done.14 = f32[3,10,1,128]{3,2,1,0:T(1,128)S(1)} collective-permute-done((f32[3,10,1,128]{3,2,1,0:T(1,128)S(1)}, f32[3,10,1,128]{3,2,1,0:T(1,128)S(1)}, u32[]{:S(2)}, u32[]{:S(2)}) %collective-permute-start.14) | collective-permute-done | bytes 15392 | tf_op jit(solution)/shard_map/ppermute | solution.py:15
  72.5 3.2 %collective-permute-start.17 = (f32[3,1,8,128]{3,2,1,0:T(8,128)S(1)}, f32[3,1,8,128]{3,2,1,0:T(8,128)S(1)}, u32[]{:S(2)}, u32[]{:S(2)}) collective-permute-start(f32[3,1,8,128]{3,2,1,0:T(8,128)S(1)} %get-tuple-element.19), channel_id=1, source_target_pairs={{0,8},{8,16},{16,24},{1,9},{9,17},{17,25},{2,10},{10,18},{18,26},{... | collective-permute-start | bytes 36872 | tf_op jit(solution)/shard_map/ppermute | solution.py:14
  79.5 4.8 %collective-permute-start.19 = (f32[3,10,1,128]{3,2,1,0:T(1,128)S(1)}, f32[3,10,1,128]{3,2,1,0:T(1,128)S(1)}, u32[]{:S(2)}, u32[]{:S(2)}) collective-permute-start(f32[3,10,1,128]{3,2,1,0:T(1,128)S(1)} %get-tuple-element.11), channel_id=1, source_target_pairs={{0,1},{1,2},{2,3},{3,4},{4,5},{5,6},{6,7},{8,9},{9,10},{10,11},{11... | collective-permute-start | bytes 46088 | tf_op jit(solution)/shard_map/ppermute | solution.py:14
  86.6 6.3 %copy.21 = f32[8,8,192,128]{3,1,2,0:T(8,128)} copy(f32[8,8,192,128]{3,2,1,0:T(8,128)S(1)} %bitcast.40) | data formatting | bytes 12582912
  94.3 17.8 %concatenate.123 = f32[64,24576]{1,0:T(8,128)} concatenate(f32[60,24576]{1,0:T(8,128)} %bitcast.38, f32[1,24576]{1,0:T(1,128)S(1)} %bitcast.42, f32[1,24576]{1,0:T(1,128)S(1)} %bitcast.43, f32[1,24576]{1,0:T(1,128)S(1)} %bitcast.44, f32[1,24576]{1,0:T(1,128)S(1)} %bitcast.45), dimensions={0} | concatenate | bytes 12582912 | tf_op jit(solution)/shard_map/concatenate | solution.py:72
  112.1 8.2 %convolution_multiply_fusion = f32[64,64]{0,1:T(8,128)S(1)} fusion(f32[64,24576]{1,0:T(8,128)} %concatenate.123), kind=kOutput, calls=%fused_computation.2 | convolution fusion | flops 1207963648 | bytes 6307840 | tf_op jit(solution)/shard_map/dot_general | solution.py:39
  120.2 42.6 %psum.7 = f32[64,64]{0,1:T(8,128)S(1)} all-reduce(f32[64,64]{0,1:T(8,128)S(1)} %convolution_multiply_fusion), channel_id=1, replica_groups=mesh['gx'=4,'gy'=8] {'gx','gy'}, use_global_device_ids=true, to_apply=%region_0.1 | all-reduce | flops 4096 | bytes 32768 | tf_op jit(solution)/shard_map/psum | solution.py:48
  163.0 5.8 %cholesky.16 = f32[64,64]{1,0:T(8,128)S(1)} custom-call(f32[64,64]{1,0:T(8,128)S(1)} %fusion.83), custom_call_target="Cholesky" | custom-call | tf_op jit(solution)/shard_map/jit(cholesky)/cholesky | solution.py:48
  170.8 4.9 %custom-call.7 = f32[1,64,64]{1,2,0:T(8,128)S(1)} custom-call(f32[1,64,64]{2,1,0:T(8,128)S(1)} %get-tuple-element.32), custom_call_target="InvertDiagBlocksLowerTriangular" | custom-call | tf_op jit(solution)/shard_map/jit(_solve_triangular)/triangular_solve | solution.py:49
  175.7 3.9 %copy.22 = f32[8,8,192,128]{3,2,1,0:T(8,128)S(1)} copy(f32[8,8,192,128]{3,1,2,0:T(8,128)} %bitcast.37) | data formatting | bytes 12582912
  179.7 9.3 %fusion = f32[64,3,8,8,128]{4,0,3,2,1:T(8,128)S(1)} fusion(f32[3,8,8,128,64]{3,2,1,0,4:T(8,128)S(1)} %bitcast.39, f32[1,64,64]{1,2,0:T(8,128)S(1)} %custom-call.7), kind=kOutput, calls=%fused_computation | convolution fusion | flops 1207959552 | bytes 12599296 | tf_op jit(solution)/shard_map/jit(_solve_triangular)/triangular_solve | solution.py:49
  189.0 6.6 %copy.16 = f32[64,3,8,8,128]{4,3,2,1,0:T(8,128)} copy(f32[64,3,8,8,128]{4,0,3,2,1:T(8,128)S(1)} %fusion) | data formatting | bytes 12582912
  (62 shorter events, 31.9 us)
Async XLA Ops:
  0.6 85.0 %copy-start = (f32[60,3,8,8,128]{4,3,2,1,0:T(8,128)S(1)}, f32[60,3,8,8,128]{4,3,2,1,0:T(8,128)}, u32[]{:S(2)}) copy-start(f32[60,3,8,8,128]{4,3,2,1,0:T(8,128)} %param.7) | copy-start | bytes 17694724
  1.5 3.9 %collective-permute-start.2 = (f32[1,8,128]{2,1,0:T(8,128)S(1)}, f32[1,8,128]{2,1,0:T(8,128)S(1)}, u32[]{:S(2)}, u32[]{:S(2)}) collective-permute-start(f32[1,8,128]{2,1,0:T(8,128)S(1)} %get-tuple-element.39), channel_id=1, source_target_pairs={{0,8},{8,16},{16,24},{1,9},{9,17},{17,25},{2,10},{10,18},{18,26},{... | collective-permute-start | bytes 12296 | tf_op jit(solution)/shard_map/ppermute | solution.py:14
  4.1 5.2 %collective-permute-start = (f32[1,8,128]{2,1,0:T(8,128)S(1)}, f32[1,8,128]{2,1,0:T(8,128)S(1)}, u32[]{:S(2)}, u32[]{:S(2)}) collective-permute-start(f32[1,8,128]{2,1,0:T(8,128)S(1)} %get-tuple-element.38), channel_id=1, source_target_pairs={{8,0},{16,8},{24,16},{9,1},{17,9},{25,17},{10,2},{18,10},{26,18},{... | collective-permute-start | bytes 12296 | tf_op jit(solution)/shard_map/ppermute | solution.py:15
  10.2 11.3 %collective-permute-start.6 = (f32[10,1,128]{2,1,0:T(1,128)S(1)}, f32[10,1,128]{2,1,0:T(1,128)S(1)}, u32[]{:S(2)}, u32[]{:S(2)}) collective-permute-start(f32[10,1,128]{2,1,0:T(1,128)S(1)} %get-tuple-element.29), channel_id=1, source_target_pairs={{0,1},{1,2},{2,3},{3,4},{4,5},{5,6},{6,7},{8,9},{9,10},{10,11},{11... | collective-permute-start | bytes 15368 | tf_op jit(solution)/shard_map/ppermute | solution.py:14
  13.6 8.0 %collective-permute-start.4 = (f32[10,1,128]{2,1,0:T(1,128)S(1)}, f32[10,1,128]{2,1,0:T(1,128)S(1)}, u32[]{:S(2)}, u32[]{:S(2)}) collective-permute-start(f32[10,1,128]{2,1,0:T(1,128)S(1)} %get-tuple-element.30), channel_id=1, source_target_pairs={{1,0},{2,1},{3,2},{4,3},{5,4},{6,5},{7,6},{9,8},{10,9},{11,10},{12... | collective-permute-start | bytes 15368 | tf_op jit(solution)/shard_map/ppermute | solution.py:15
  15.6 7.6 %collective-permute-start.1 = (f32[3,1,8,128]{3,2,1,0:T(8,128)S(1)}, f32[3,1,8,128]{3,2,1,0:T(8,128)S(1)}, u32[]{:S(2)}, u32[]{:S(2)}) collective-permute-start(f32[3,1,8,128]{3,2,1,0:T(8,128)S(1)} %get-tuple-element.25), channel_id=1, source_target_pairs={{8,0},{16,8},{24,16},{9,1},{17,9},{25,17},{10,2},{18,10},{26,18},{... | collective-permute-start | bytes 36872 | tf_op jit(solution)/shard_map/ppermute | solution.py:15
  16.9 5.4 %collective-permute-start.3 = (f32[3,1,8,128]{3,2,1,0:T(8,128)S(1)}, f32[3,1,8,128]{3,2,1,0:T(8,128)S(1)}, u32[]{:S(2)}, u32[]{:S(2)}) collective-permute-start(f32[3,1,8,128]{3,2,1,0:T(8,128)S(1)} %get-tuple-element.26), channel_id=1, source_target_pairs={{0,8},{8,16},{16,24},{1,9},{9,17},{17,25},{2,10},{10,18},{18,26},{... | collective-permute-start | bytes 36872 | tf_op jit(solution)/shard_map/ppermute | solution.py:14
  23.3 6.4 %collective-permute-start.7 = (f32[3,10,1,128]{3,2,1,0:T(1,128)S(1)}, f32[3,10,1,128]{3,2,1,0:T(1,128)S(1)}, u32[]{:S(2)}, u32[]{:S(2)}) collective-permute-start(f32[3,10,1,128]{3,2,1,0:T(1,128)S(1)} %get-tuple-element.17), channel_id=1, source_target_pairs={{0,1},{1,2},{2,3},{3,4},{4,5},{5,6},{6,7},{8,9},{9,10},{10,11},{11... | collective-permute-start | bytes 46088 | tf_op jit(solution)/shard_map/ppermute | solution.py:14
  27.6 6.1 %collective-permute-start.5 = (f32[3,10,1,128]{3,2,1,0:T(1,128)S(1)}, f32[3,10,1,128]{3,2,1,0:T(1,128)S(1)}, u32[]{:S(2)}, u32[]{:S(2)}) collective-permute-start(f32[3,10,1,128]{3,2,1,0:T(1,128)S(1)} %get-tuple-element.18), channel_id=1, source_target_pairs={{1,0},{2,1},{3,2},{4,3},{5,4},{6,5},{7,6},{9,8},{10,9},{11,10},{12... | collective-permute-start | bytes 46088 | tf_op jit(solution)/shard_map/ppermute | solution.py:15
  35.2 3.8 %collective-permute-start.9 = (f32[3,1,8,128]{3,2,1,0:T(8,128)S(1)}, f32[3,1,8,128]{3,2,1,0:T(8,128)S(1)}, u32[]{:S(2)}, u32[]{:S(2)}) collective-permute-start(f32[3,1,8,128]{3,2,1,0:T(8,128)S(1)} %get-tuple-element.23), channel_id=1, source_target_pairs={{0,8},{8,16},{16,24},{1,9},{9,17},{17,25},{2,10},{10,18},{18,26},{... | collective-permute-start | bytes 36872 | tf_op jit(solution)/shard_map/ppermute | solution.py:14
  37.7 6.0 %collective-permute-start.8 = (f32[3,1,8,128]{3,2,1,0:T(8,128)S(1)}, f32[3,1,8,128]{3,2,1,0:T(8,128)S(1)}, u32[]{:S(2)}, u32[]{:S(2)}) collective-permute-start(f32[3,1,8,128]{3,2,1,0:T(8,128)S(1)} %get-tuple-element.24), channel_id=1, source_target_pairs={{8,0},{16,8},{24,16},{9,1},{17,9},{25,17},{10,2},{18,10},{26,18},{... | collective-permute-start | bytes 36872 | tf_op jit(solution)/shard_map/ppermute | solution.py:15
  43.7 6.2 %collective-permute-start.11 = (f32[3,10,1,128]{3,2,1,0:T(1,128)S(1)}, f32[3,10,1,128]{3,2,1,0:T(1,128)S(1)}, u32[]{:S(2)}, u32[]{:S(2)}) collective-permute-start(f32[3,10,1,128]{3,2,1,0:T(1,128)S(1)} %get-tuple-element.15), channel_id=1, source_target_pairs={{0,1},{1,2},{2,3},{3,4},{4,5},{5,6},{6,7},{8,9},{9,10},{10,11},{11... | collective-permute-start | bytes 46088 | tf_op jit(solution)/shard_map/ppermute | solution.py:14
  48.6 5.6 %collective-permute-start.10 = (f32[3,10,1,128]{3,2,1,0:T(1,128)S(1)}, f32[3,10,1,128]{3,2,1,0:T(1,128)S(1)}, u32[]{:S(2)}, u32[]{:S(2)}) collective-permute-start(f32[3,10,1,128]{3,2,1,0:T(1,128)S(1)} %get-tuple-element.16), channel_id=1, source_target_pairs={{1,0},{2,1},{3,2},{4,3},{5,4},{6,5},{7,6},{9,8},{10,9},{11,10},{12... | collective-permute-start | bytes 46088 | tf_op jit(solution)/shard_map/ppermute | solution.py:15
  55.6 4.2 %collective-permute-start.13 = (f32[3,1,8,128]{3,2,1,0:T(8,128)S(1)}, f32[3,1,8,128]{3,2,1,0:T(8,128)S(1)}, u32[]{:S(2)}, u32[]{:S(2)}) collective-permute-start(f32[3,1,8,128]{3,2,1,0:T(8,128)S(1)} %get-tuple-element.21), channel_id=1, source_target_pairs={{0,8},{8,16},{16,24},{1,9},{9,17},{17,25},{2,10},{10,18},{18,26},{... | collective-permute-start | bytes 36872 | tf_op jit(solution)/shard_map/ppermute | solution.py:14
  58.5 4.0 %collective-permute-start.12 = (f32[3,1,8,128]{3,2,1,0:T(8,128)S(1)}, f32[3,1,8,128]{3,2,1,0:T(8,128)S(1)}, u32[]{:S(2)}, u32[]{:S(2)}) collective-permute-start(f32[3,1,8,128]{3,2,1,0:T(8,128)S(1)} %get-tuple-element.22), channel_id=1, source_target_pairs={{8,0},{16,8},{24,16},{9,1},{17,9},{25,17},{10,2},{18,10},{26,18},{... | collective-permute-start | bytes 36872 | tf_op jit(solution)/shard_map/ppermute | solution.py:15
  62.5 4.4 %collective-permute-start.15 = (f32[3,10,1,128]{3,2,1,0:T(1,128)S(1)}, f32[3,10,1,128]{3,2,1,0:T(1,128)S(1)}, u32[]{:S(2)}, u32[]{:S(2)}) collective-permute-start(f32[3,10,1,128]{3,2,1,0:T(1,128)S(1)} %get-tuple-element.13), channel_id=1, source_target_pairs={{0,1},{1,2},{2,3},{3,4},{4,5},{5,6},{6,7},{8,9},{9,10},{10,11},{11... | collective-permute-start | bytes 46088 | tf_op jit(solution)/shard_map/ppermute | solution.py:14
  65.5 5.6 %collective-permute-start.14 = (f32[3,10,1,128]{3,2,1,0:T(1,128)S(1)}, f32[3,10,1,128]{3,2,1,0:T(1,128)S(1)}, u32[]{:S(2)}, u32[]{:S(2)}) collective-permute-start(f32[3,10,1,128]{3,2,1,0:T(1,128)S(1)} %get-tuple-element.14), channel_id=1, source_target_pairs={{1,0},{2,1},{3,2},{4,3},{5,4},{6,5},{7,6},{9,8},{10,9},{11,10},{12... | collective-permute-start | bytes 46088 | tf_op jit(solution)/shard_map/ppermute | solution.py:15
  72.5 4.5 %collective-permute-start.17 = (f32[3,1,8,128]{3,2,1,0:T(8,128)S(1)}, f32[3,1,8,128]{3,2,1,0:T(8,128)S(1)}, u32[]{:S(2)}, u32[]{:S(2)}) collective-permute-start(f32[3,1,8,128]{3,2,1,0:T(8,128)S(1)} %get-tuple-element.19), channel_id=1, source_target_pairs={{0,8},{8,16},{16,24},{1,9},{9,17},{17,25},{2,10},{10,18},{18,26},{... | collective-permute-start | bytes 36872 | tf_op jit(solution)/shard_map/ppermute | solution.py:14
  75.7 3.8 %collective-permute-start.16 = (f32[3,1,8,128]{3,2,1,0:T(8,128)S(1)}, f32[3,1,8,128]{3,2,1,0:T(8,128)S(1)}, u32[]{:S(2)}, u32[]{:S(2)}) collective-permute-start(f32[3,1,8,128]{3,2,1,0:T(8,128)S(1)} %get-tuple-element.20), channel_id=1, source_target_pairs={{8,0},{16,8},{24,16},{9,1},{17,9},{25,17},{10,2},{18,10},{26,18},{... | collective-permute-start | bytes 36872 | tf_op jit(solution)/shard_map/ppermute | solution.py:15
  79.5 13.4 %collective-permute-start.19 = (f32[3,10,1,128]{3,2,1,0:T(1,128)S(1)}, f32[3,10,1,128]{3,2,1,0:T(1,128)S(1)}, u32[]{:S(2)}, u32[]{:S(2)}) collective-permute-start(f32[3,10,1,128]{3,2,1,0:T(1,128)S(1)} %get-tuple-element.11), channel_id=1, source_target_pairs={{0,1},{1,2},{2,3},{3,4},{4,5},{5,6},{6,7},{8,9},{9,10},{10,11},{11... | collective-permute-start | bytes 46088 | tf_op jit(solution)/shard_map/ppermute | solution.py:14
  84.3 8.6 %collective-permute-start.18 = (f32[3,10,1,128]{3,2,1,0:T(1,128)S(1)}, f32[3,10,1,128]{3,2,1,0:T(1,128)S(1)}, u32[]{:S(2)}, u32[]{:S(2)}) collective-permute-start(f32[3,10,1,128]{3,2,1,0:T(1,128)S(1)} %get-tuple-element.12), channel_id=1, source_target_pairs={{1,0},{2,1},{3,2},{4,3},{5,4},{6,5},{7,6},{9,8},{10,9},{11,10},{12... | collective-permute-start | bytes 46088 | tf_op jit(solution)/shard_map/ppermute | solution.py:15
  94.3 17.8 %copy-start.1 = (f32[3,8,8,128]{3,2,1,0:T(8,128)}, f32[3,8,8,128]{3,2,1,0:T(8,128)S(1)}, u32[]{:S(2)}) copy-start(f32[3,8,8,128]{3,2,1,0:T(8,128)S(1)} %fusion.7) | copy-start | bytes 294916
where the time goes:
time: 197 us; the launch traced here: 196 us
  starting transfers between devices  49 us (25%)
  blocking collectives  42.6 us (22%)
  local copies, waits for them, and re-layouts  38.9 us (20%)
  waiting for transfers between devices  27 us (14%)
  other arithmetic  19.6 us (10%)
  matrix products  17.5 us (9%)
    psum x1, blocking collectives, factorize(): lower_factor = jnp.linalg.cholesky(lax.psum(local_gram, ('gx', 'gy')))  42.6 us
    ppermute x10, starting transfers between devices, padded_2(): before = lax.ppermute(last, axis, up)  36.1 us
    ppermute x10, waiting for transfers between devices, padded_2(): after = lax.ppermute(initial, axis, down)  26.1 us
    unnamed x12, local copies, waits for them, and re-layouts  19.4 us
    concatenate x1, local copies, waits for them, and re-layouts, local(): jnp.concatenate([panel_old] + snapshots, 0)  17.8 us
    ppermute x10, starting transfers between devices, padded_2(): after = lax.ppermute(initial, axis, down)  12.9 us
    another operation x1, matrix products, factorize(): basis = jax.scipy.linalg.solve_triangular(lower_factor, panel, lower=True)  9.33 us
    dot_general x1, matrix products, factorize(): lax.dot_general(panel, panel, (((1,), (1,)), ((), ())), precision=lax.Pre...  8.18 us
  transfers between devices with their start and end apart: 20, of which 10 were waited for; matrix products, arithmetic and copies ran while one was open for 5% of the time, Pallas kernels for 0%

commit v1 on v0

--- a/solution.py
+++ b/solution.py
@@ -2,6 +2,11 @@
 import jax.numpy as jnp
 from jax import lax
 from jax.sharding import PartitionSpec as P
+
+
+def summed_here(block, name):
+    parts = lax.all_gather(block, name)
+    return jnp.sum(parts, axis=0)
 
 
 def padded_2(array, sides, width):
@@ -45,7 +50,7 @@
         )
         / total_rows
     )
-    lower_factor = jnp.linalg.cholesky(lax.psum(local_gram, ("gx", "gy")))
+    lower_factor = jnp.linalg.cholesky(summed_here(local_gram, ("gx", "gy")))
     basis = jax.scipy.linalg.solve_triangular(lower_factor, panel, lower=True)
     return (lower_factor, basis)
 

time: 197 us -> 227 us (1.15)
  blocking collectives: 42.6 us -> 72.8 us
    all_gather x0 -> x1, blocking collectives: none -> 72.8 us  [summed_here(): parts = lax.all_gather(block, name)]
    psum x1 -> x0, blocking collectives: 42.6 us -> none  [factorize(): lower_factor = jnp.linalg.cholesky(lax.psum(local_gram, ('gx', 'gy')))]
  transfers between devices with their start and end apart: 20 -> 20, of which waited for: 10 -> 10; matrix products, arithmetic and copies ran while one was open for 5% -> 4% of each run, Pallas kernels for 0% -> 0%
where the time goes in v1:
time: 227 us; the launch traced here: 226 us
  blocking collectives  72.8 us (32%)
  starting transfers between devices  49 us (22%)
  local copies, waits for them, and re-layouts  38.6 us (17%)
  waiting for transfers between devices  27 us (12%)
  other arithmetic  19.7 us (9%)
  matrix products  17.5 us (8%)
    all_gather x1, blocking collectives, summed_here(): parts = lax.all_gather(block, name)  72.8 us
    ppermute x10, starting transfers between devices, padded_2(): before = lax.ppermute(last, axis, up)  36.1 us
    ppermute x10, waiting for transfers between devices, padded_2(): after = lax.ppermute(initial, axis, down)  26.1 us
    unnamed x12, local copies, waits for them, and re-layouts  19.1 us
    concatenate x1, local copies, waits for them, and re-layouts, local(): jnp.concatenate([panel_old] + snapshots, 0)  17.8 us
    ppermute x10, starting transfers between devices, padded_2(): after = lax.ppermute(initial, axis, down)  12.9 us
    another operation x1, matrix products, factorize(): basis = jax.scipy.linalg.solve_triangular(lower_factor, panel, lower=True)  9.33 us
    dot_general x1, matrix products, factorize(): lax.dot_general(panel, panel, (((1,), (1,)), ((), ())), precision=lax.Pre...  8.16 us
  transfers between devices with their start and end apart: 20, of which 10 were waited for; matrix products, arithmetic and copies ran while one was open for 4% of the time, Pallas kernels for 0%

profile of v1, /device:TPU:0, one launch (start us, length us, event | category | flops | bytes accessed | tf_op | source)
XLA Modules:
  0.0 225.8 jit_solution(3379607018065146620)
XLA Ops:
  1.5 2.6 %collective-permute-start.2 = (f32[1,8,128]{2,1,0:T(8,128)S(1)}, f32[1,8,128]{2,1,0:T(8,128)S(1)}, u32[]{:S(2)}, u32[]{:S(2)}) collective-permute-start(f32[1,8,128]{2,1,0:T(8,128)S(1)} %get-tuple-element.42), channel_id=1, source_target_pairs={{0,8},{8,16},{16,24},{1,9},{9,17},{17,25},{2,10},{10,18},{18,26},{... | collective-permute-start | bytes 12296 | tf_op jit(solution)/shard_map/ppermute | solution.py:19
  5.4 3.9 %collective-permute-done = f32[1,8,128]{2,1,0:T(8,128)S(1)} collective-permute-done((f32[1,8,128]{2,1,0:T(8,128)S(1)}, f32[1,8,128]{2,1,0:T(8,128)S(1)}, u32[]{:S(2)}, u32[]{:S(2)}) %collective-permute-start) | collective-permute-done | bytes 4128 | tf_op jit(solution)/shard_map/ppermute | solution.py:20
  10.2 3.4 %collective-permute-start.6 = (f32[10,1,128]{2,1,0:T(1,128)S(1)}, f32[10,1,128]{2,1,0:T(1,128)S(1)}, u32[]{:S(2)}, u32[]{:S(2)}) collective-permute-start(f32[10,1,128]{2,1,0:T(1,128)S(1)} %get-tuple-element.32), channel_id=1, source_target_pairs={{0,1},{1,2},{2,3},{3,4},{4,5},{5,6},{6,7},{8,9},{9,10},{10,11},{11... | collective-permute-start | bytes 15368 | tf_op jit(solution)/shard_map/ppermute | solution.py:19
  16.9 4.6 %collective-permute-start.3 = (f32[3,1,8,128]{3,2,1,0:T(8,128)S(1)}, f32[3,1,8,128]{3,2,1,0:T(8,128)S(1)}, u32[]{:S(2)}, u32[]{:S(2)}) collective-permute-start(f32[3,1,8,128]{3,2,1,0:T(8,128)S(1)} %get-tuple-element.29), channel_id=1, source_target_pairs={{0,8},{8,16},{16,24},{1,9},{9,17},{17,25},{2,10},{10,18},{18,26},{... | collective-permute-start | bytes 36872 | tf_op jit(solution)/shard_map/ppermute | solution.py:19
  23.3 4.3 %collective-permute-start.7 = (f32[3,10,1,128]{3,2,1,0:T(1,128)S(1)}, f32[3,10,1,128]{3,2,1,0:T(1,128)S(1)}, u32[]{:S(2)}, u32[]{:S(2)}) collective-permute-start(f32[3,10,1,128]{3,2,1,0:T(1,128)S(1)} %get-tuple-element.20), channel_id=1, source_target_pairs={{0,1},{1,2},{2,3},{3,4},{4,5},{5,6},{6,7},{8,9},{9,10},{10,11},{11... | collective-permute-start | bytes 46088 | tf_op jit(solution)/shard_map/ppermute | solution.py:19
  29.8 3.9 %collective-permute-done.5 = f32[3,10,1,128]{3,2,1,0:T(1,128)S(1)} collective-permute-done((f32[3,10,1,128]{3,2,1,0:T(1,128)S(1)}, f32[3,10,1,128]{3,2,1,0:T(1,128)S(1)}, u32[]{:S(2)}, u32[]{:S(2)}) %collective-permute-start.5) | collective-permute-done | bytes 15392 | tf_op jit(solution)/shard_map/ppermute | solution.py:20
  39.0 4.7 %collective-permute-done.8 = f32[3,1,8,128]{3,2,1,0:T(8,128)S(1)} collective-permute-done((f32[3,1,8,128]{3,2,1,0:T(8,128)S(1)}, f32[3,1,8,128]{3,2,1,0:T(8,128)S(1)}, u32[]{:S(2)}, u32[]{:S(2)}) %collective-permute-start.8) | collective-permute-done | bytes 12320 | tf_op jit(solution)/shard_map/ppermute | solution.py:20
  43.7 4.8 %collective-permute-start.11 = (f32[3,10,1,128]{3,2,1,0:T(1,128)S(1)}, f32[3,10,1,128]{3,2,1,0:T(1,128)S(1)}, u32[]{:S(2)}, u32[]{:S(2)}) collective-permute-start(f32[3,10,1,128]{3,2,1,0:T(1,128)S(1)} %get-tuple-element.18), channel_id=1, source_target_pairs={{0,1},{1,2},{2,3},{3,4},{4,5},{5,6},{6,7},{8,9},{9,10},{10,11},{11... | collective-permute-start | bytes 46088 | tf_op jit(solution)/shard_map/ppermute | solution.py:19
  50.0 4.2 %collective-permute-done.10 = f32[3,10,1,128]{3,2,1,0:T(1,128)S(1)} collective-permute-done((f32[3,10,1,128]{3,2,1,0:T(1,128)S(1)}, f32[3,10,1,128]{3,2,1,0:T(1,128)S(1)}, u32[]{:S(2)}, u32[]{:S(2)}) %collective-permute-start.10) | collective-permute-done | bytes 15392 | tf_op jit(solution)/shard_map/ppermute | solution.py:20
  55.6 2.9 %collective-permute-start.13 = (f32[3,1,8,128]{3,2,1,0:T(8,128)S(1)}, f32[3,1,8,128]{3,2,1,0:T(8,128)S(1)}, u32[]{:S(2)}, u32[]{:S(2)}) collective-permute-start(f32[3,1,8,128]{3,2,1,0:T(8,128)S(1)} %get-tuple-element.24), channel_id=1, source_target_pairs={{0,8},{8,16},{16,24},{1,9},{9,17},{17,25},{2,10},{10,18},{18,26},{... | collective-permute-start | bytes 36872 | tf_op jit(solution)/shard_map/ppermute | solution.py:19
  59.8 2.7 %collective-permute-done.12 = f32[3,1,8,128]{3,2,1,0:T(8,128)S(1)} collective-permute-done((f32[3,1,8,128]{3,2,1,0:T(8,128)S(1)}, f32[3,1,8,128]{3,2,1,0:T(8,128)S(1)}, u32[]{:S(2)}, u32[]{:S(2)}) %collective-permute-start.12) | collective-permute-done | bytes 12320 | tf_op jit(solution)/shard_map/ppermute | solution.py:20
  62.5 2.9 %collective-permute-start.15 = (f32[3,10,1,128]{3,2,1,0:T(1,128)S(1)}, f32[3,10,1,128]{3,2,1,0:T(1,128)S(1)}, u32[]{:S(2)}, u32[]{:S(2)}) collective-permute-start(f32[3,10,1,128]{3,2,1,0:T(1,128)S(1)} %get-tuple-element.16), channel_id=1, source_target_pairs={{0,1},{1,2},{2,3},{3,4},{4,5},{5,6},{6,7},{8,9},{9,10},{10,11},{11... | collective-permute-start | bytes 46088 | tf_op jit(solution)/shard_map/ppermute | solution.py:19
  66.9 4.2 %collective-permute-done.14 = f32[3,10,1,128]{3,2,1,0:T(1,128)S(1)} collective-permute-done((f32[3,10,1,128]{3,2,1,0:T(1,128)S(1)}, f32[3,10,1,128]{3,2,1,0:T(1,128)S(1)}, u32[]{:S(2)}, u32[]{:S(2)}) %collective-permute-start.14) | collective-permute-done | bytes 15392 | tf_op jit(solution)/shard_map/ppermute | solution.py:20
  72.5 3.2 %collective-permute-start.17 = (f32[3,1,8,128]{3,2,1,0:T(8,128)S(1)}, f32[3,1,8,128]{3,2,1,0:T(8,128)S(1)}, u32[]{:S(2)}, u32[]{:S(2)}) collective-permute-start(f32[3,1,8,128]{3,2,1,0:T(8,128)S(1)} %get-tuple-element.22), channel_id=1, source_target_pairs={{0,8},{8,16},{16,24},{1,9},{9,17},{17,25},{2,10},{10,18},{18,26},{... | collective-permute-start | bytes 36872 | tf_op jit(solution)/shard_map/ppermute | solution.py:19
  79.5 4.8 %collective-permute-start.19 = (f32[3,10,1,128]{3,2,1,0:T(1,128)S(1)}, f32[3,10,1,128]{3,2,1,0:T(1,128)S(1)}, u32[]{:S(2)}, u32[]{:S(2)}) collective-permute-start(f32[3,10,1,128]{3,2,1,0:T(1,128)S(1)} %get-tuple-element.14), channel_id=1, source_target_pairs={{0,1},{1,2},{2,3},{3,4},{4,5},{5,6},{6,7},{8,9},{9,10},{10,11},{11... | collective-permute-start | bytes 46088 | tf_op jit(solution)/shard_map/ppermute | solution.py:19
  86.6 6.3 %copy.23 = f32[8,8,192,128]{3,1,2,0:T(8,128)} copy(f32[8,8,192,128]{3,2,1,0:T(8,128)S(1)} %bitcast.41) | data formatting | bytes 12582912
  94.3 17.8 %concatenate.123 = f32[64,24576]{1,0:T(8,128)} concatenate(f32[60,24576]{1,0:T(8,128)} %bitcast.39, f32[1,24576]{1,0:T(1,128)S(1)} %bitcast.44, f32[1,24576]{1,0:T(1,128)S(1)} %bitcast.45, f32[1,24576]{1,0:T(1,128)S(1)} %bitcast.46, f32[1,24576]{1,0:T(1,128)S(1)} %bitcast.47), dimensions={0} | concatenate | bytes 12582912 | tf_op jit(solution)/shard_map/concatenate | solution.py:77
  112.1 8.2 %convolution_multiply_fusion = f32[64,64]{1,0:T(8,128)S(1)} fusion(f32[64,24576]{1,0:T(8,128)} %concatenate.123), kind=kOutput, calls=%fused_computation.2 | convolution fusion | flops 1207963648 | bytes 6307840 | tf_op jit(solution)/shard_map/dot_general | solution.py:44
  120.2 72.8 %all-gather = f32[2048,64]{1,0:T(8,128)S(1)} all-gather(f32[64,64]{1,0:T(8,128)S(1)} %convolution_multiply_fusion), channel_id=2, replica_groups=mesh['gx'=4,'gy'=8] {'gx','gy'}, dimensions={0}, use_global_device_ids=true | all-gather | bytes 540672 | tf_op jit(solution)/shard_map/all_gather | solution.py:8
  193.2 5.8 %cholesky.16 = f32[64,64]{1,0:T(8,128)S(1)} custom-call(f32[64,64]{1,0:T(8,128)S(1)} %fusion.83), custom_call_target="Cholesky" | custom-call | tf_op jit(solution)/shard_map/jit(cholesky)/cholesky | solution.py:53
  201.1 4.9 %custom-call.7 = f32[1,64,64]{1,2,0:T(8,128)S(1)} custom-call(f32[1,64,64]{2,1,0:T(8,128)S(1)} %get-tuple-element.35), custom_call_target="InvertDiagBlocksLowerTriangular" | custom-call | tf_op jit(solution)/shard_map/jit(_solve_triangular)/triangular_solve | solution.py:54
  206.0 3.9 %copy.24 = f32[8,8,192,128]{3,2,1,0:T(8,128)S(1)} copy(f32[8,8,192,128]{3,1,2,0:T(8,128)} %bitcast.38) | data formatting | bytes 12582912
  209.9 9.3 %fusion = f32[64,3,8,8,128]{4,0,3,2,1:T(8,128)S(1)} fusion(f32[3,8,8,128,64]{3,2,1,0,4:T(8,128)S(1)} %bitcast.40, f32[1,64,64]{1,2,0:T(8,128)S(1)} %custom-call.7), kind=kOutput, calls=%fused_computation | convolution fusion | flops 1207959552 | bytes 12599296 | tf_op jit(solution)/shard_map/jit(_solve_triangular)/triangular_solve | solution.py:54
  219.5 6.3 %copy.19 = f32[64,3,8,8,128]{4,3,2,1,0:T(8,128)} copy(f32[64,3,8,8,128]{4,0,3,2,1:T(8,128)S(1)} %fusion) | data formatting | bytes 12582912
  (63 shorter events, 32.0 us)
Async XLA Ops:
  0.6 85.0 %copy-start = (f32[60,3,8,8,128]{4,3,2,1,0:T(8,128)S(1)}, f32[60,3,8,8,128]{4,3,2,1,0:T(8,128)}, u32[]{:S(2)}) copy-start(f32[60,3,8,8,128]{4,3,2,1,0:T(8,128)} %param.7) | copy-start | bytes 17694724
  1.5 3.9 %collective-permute-start.2 = (f32[1,8,128]{2,1,0:T(8,128)S(1)}, f32[1,8,128]{2,1,0:T(8,128)S(1)}, u32[]{:S(2)}, u32[]{:S(2)}) collective-permute-start(f32[1,8,128]{2,1,0:T(8,128)S(1)} %get-tuple-element.42), channel_id=1, source_target_pairs={{0,8},{8,16},{16,24},{1,9},{9,17},{17,25},{2,10},{10,18},{18,26},{... | collective-permute-start | bytes 12296 | tf_op jit(solution)/shard_map/ppermute | solution.py:19
  4.1 5.2 %collective-permute-start = (f32[1,8,128]{2,1,0:T(8,128)S(1)}, f32[1,8,128]{2,1,0:T(8,128)S(1)}, u32[]{:S(2)}, u32[]{:S(2)}) collective-permute-start(f32[1,8,128]{2,1,0:T(8,128)S(1)} %get-tuple-element.41), channel_id=1, source_target_pairs={{8,0},{16,8},{24,16},{9,1},{17,9},{25,17},{10,2},{18,10},{26,18},{... | collective-permute-start | bytes 12296 | tf_op jit(solution)/shard_map/ppermute | solution.py:20
  10.2 11.3 %collective-permute-start.6 = (f32[10,1,128]{2,1,0:T(1,128)S(1)}, f32[10,1,128]{2,1,0:T(1,128)S(1)}, u32[]{:S(2)}, u32[]{:S(2)}) collective-permute-start(f32[10,1,128]{2,1,0:T(1,128)S(1)} %get-tuple-element.32), channel_id=1, source_target_pairs={{0,1},{1,2},{2,3},{3,4},{4,5},{5,6},{6,7},{8,9},{9,10},{10,11},{11... | collective-permute-start | bytes 15368 | tf_op jit(solution)/shard_map/ppermute | solution.py:19
  13.6 8.0 %collective-permute-start.4 = (f32[10,1,128]{2,1,0:T(1,128)S(1)}, f32[10,1,128]{2,1,0:T(1,128)S(1)}, u32[]{:S(2)}, u32[]{:S(2)}) collective-permute-start(f32[10,1,128]{2,1,0:T(1,128)S(1)} %get-tuple-element.33), channel_id=1, source_target_pairs={{1,0},{2,1},{3,2},{4,3},{5,4},{6,5},{7,6},{9,8},{10,9},{11,10},{12... | collective-permute-start | bytes 15368 | tf_op jit(solution)/shard_map/ppermute | solution.py:20
  15.6 7.6 %collective-permute-start.1 = (f32[3,1,8,128]{3,2,1,0:T(8,128)S(1)}, f32[3,1,8,128]{3,2,1,0:T(8,128)S(1)}, u32[]{:S(2)}, u32[]{:S(2)}) collective-permute-start(f32[3,1,8,128]{3,2,1,0:T(8,128)S(1)} %get-tuple-element.28), channel_id=1, source_target_pairs={{8,0},{16,8},{24,16},{9,1},{17,9},{25,17},{10,2},{18,10},{26,18},{... | collective-permute-start | bytes 36872 | tf_op jit(solution)/shard_map/ppermute | solution.py:20
  16.9 5.4 %collective-permute-start.3 = (f32[3,1,8,128]{3,2,1,0:T(8,128)S(1)}, f32[3,1,8,128]{3,2,1,0:T(8,128)S(1)}, u32[]{:S(2)}, u32[]{:S(2)}) collective-permute-start(f32[3,1,8,128]{3,2,1,0:T(8,128)S(1)} %get-tuple-element.29), channel_id=1, source_target_pairs={{0,8},{8,16},{16,24},{1,9},{9,17},{17,25},{2,10},{10,18},{18,26},{... | collective-permute-start | bytes 36872 | tf_op jit(solution)/shard_map/ppermute | solution.py:19
  23.3 6.4 %collective-permute-start.7 = (f32[3,10,1,128]{3,2,1,0:T(1,128)S(1)}, f32[3,10,1,128]{3,2,1,0:T(1,128)S(1)}, u32[]{:S(2)}, u32[]{:S(2)}) collective-permute-start(f32[3,10,1,128]{3,2,1,0:T(1,128)S(1)} %get-tuple-element.20), channel_id=1, source_target_pairs={{0,1},{1,2},{2,3},{3,4},{4,5},{5,6},{6,7},{8,9},{9,10},{10,11},{11... | collective-permute-start | bytes 46088 | tf_op jit(solution)/shard_map/ppermute | solution.py:19
  27.6 6.1 %collective-permute-start.5 = (f32[3,10,1,128]{3,2,1,0:T(1,128)S(1)}, f32[3,10,1,128]{3,2,1,0:T(1,128)S(1)}, u32[]{:S(2)}, u32[]{:S(2)}) collective-permute-start(f32[3,10,1,128]{3,2,1,0:T(1,128)S(1)} %get-tuple-element.21), channel_id=1, source_target_pairs={{1,0},{2,1},{3,2},{4,3},{5,4},{6,5},{7,6},{9,8},{10,9},{11,10},{12... | collective-permute-start | bytes 46088 | tf_op jit(solution)/shard_map/ppermute | solution.py:20
  35.2 3.8 %collective-permute-start.9 = (f32[3,1,8,128]{3,2,1,0:T(8,128)S(1)}, f32[3,1,8,128]{3,2,1,0:T(8,128)S(1)}, u32[]{:S(2)}, u32[]{:S(2)}) collective-permute-start(f32[3,1,8,128]{3,2,1,0:T(8,128)S(1)} %get-tuple-element.26), channel_id=1, source_target_pairs={{0,8},{8,16},{16,24},{1,9},{9,17},{17,25},{2,10},{10,18},{18,26},{... | collective-permute-start | bytes 36872 | tf_op jit(solution)/shard_map/ppermute | solution.py:19
  37.7 6.0 %collective-permute-start.8 = (f32[3,1,8,128]{3,2,1,0:T(8,128)S(1)}, f32[3,1,8,128]{3,2,1,0:T(8,128)S(1)}, u32[]{:S(2)}, u32[]{:S(2)}) collective-permute-start(f32[3,1,8,128]{3,2,1,0:T(8,128)S(1)} %get-tuple-element.27), channel_id=1, source_target_pairs={{8,0},{16,8},{24,16},{9,1},{17,9},{25,17},{10,2},{18,10},{26,18},{... | collective-permute-start | bytes 36872 | tf_op jit(solution)/shard_map/ppermute | solution.py:20
  43.7 6.2 %collective-permute-start.11 = (f32[3,10,1,128]{3,2,1,0:T(1,128)S(1)}, f32[3,10,1,128]{3,2,1,0:T(1,128)S(1)}, u32[]{:S(2)}, u32[]{:S(2)}) collective-permute-start(f32[3,10,1,128]{3,2,1,0:T(1,128)S(1)} %get-tuple-element.18), channel_id=1, source_target_pairs={{0,1},{1,2},{2,3},{3,4},{4,5},{5,6},{6,7},{8,9},{9,10},{10,11},{11... | collective-permute-start | bytes 46088 | tf_op jit(solution)/shard_map/ppermute | solution.py:19
  48.6 5.6 %collective-permute-start.10 = (f32[3,10,1,128]{3,2,1,0:T(1,128)S(1)}, f32[3,10,1,128]{3,2,1,0:T(1,128)S(1)}, u32[]{:S(2)}, u32[]{:S(2)}) collective-permute-start(f32[3,10,1,128]{3,2,1,0:T(1,128)S(1)} %get-tuple-element.19), channel_id=1, source_target_pairs={{1,0},{2,1},{3,2},{4,3},{5,4},{6,5},{7,6},{9,8},{10,9},{11,10},{12... | collective-permute-start | bytes 46088 | tf_op jit(solution)/shard_map/ppermute | solution.py:20
  55.6 4.2 %collective-permute-start.13 = (f32[3,1,8,128]{3,2,1,0:T(8,128)S(1)}, f32[3,1,8,128]{3,2,1,0:T(8,128)S(1)}, u32[]{:S(2)}, u32[]{:S(2)}) collective-permute-start(f32[3,1,8,128]{3,2,1,0:T(8,128)S(1)} %get-tuple-element.24), channel_id=1, source_target_pairs={{0,8},{8,16},{16,24},{1,9},{9,17},{17,25},{2,10},{10,18},{18,26},{... | collective-permute-start | bytes 36872 | tf_op jit(solution)/shard_map/ppermute | solution.py:19
  58.5 4.0 %collective-permute-start.12 = (f32[3,1,8,128]{3,2,1,0:T(8,128)S(1)}, f32[3,1,8,128]{3,2,1,0:T(8,128)S(1)}, u32[]{:S(2)}, u32[]{:S(2)}) collective-permute-start(f32[3,1,8,128]{3,2,1,0:T(8,128)S(1)} %get-tuple-element.25), channel_id=1, source_target_pairs={{8,0},{16,8},{24,16},{9,1},{17,9},{25,17},{10,2},{18,10},{26,18},{... | collective-permute-start | bytes 36872 | tf_op jit(solution)/shard_map/ppermute | solution.py:20
  62.5 4.4 %collective-permute-start.15 = (f32[3,10,1,128]{3,2,1,0:T(1,128)S(1)}, f32[3,10,1,128]{3,2,1,0:T(1,128)S(1)}, u32[]{:S(2)}, u32[]{:S(2)}) collective-permute-start(f32[3,10,1,128]{3,2,1,0:T(1,128)S(1)} %get-tuple-element.16), channel_id=1, source_target_pairs={{0,1},{1,2},{2,3},{3,4},{4,5},{5,6},{6,7},{8,9},{9,10},{10,11},{11... | collective-permute-start | bytes 46088 | tf_op jit(solution)/shard_map/ppermute | solution.py:19
  65.5 5.6 %collective-permute-start.14 = (f32[3,10,1,128]{3,2,1,0:T(1,128)S(1)}, f32[3,10,1,128]{3,2,1,0:T(1,128)S(1)}, u32[]{:S(2)}, u32[]{:S(2)}) collective-permute-start(f32[3,10,1,128]{3,2,1,0:T(1,128)S(1)} %get-tuple-element.17), channel_id=1, source_target_pairs={{1,0},{2,1},{3,2},{4,3},{5,4},{6,5},{7,6},{9,8},{10,9},{11,10},{12... | collective-permute-start | bytes 46088 | tf_op jit(solution)/shard_map/ppermute | solution.py:20
  72.5 4.5 %collective-permute-start.17 = (f32[3,1,8,128]{3,2,1,0:T(8,128)S(1)}, f32[3,1,8,128]{3,2,1,0:T(8,128)S(1)}, u32[]{:S(2)}, u32[]{:S(2)}) collective-permute-start(f32[3,1,8,128]{3,2,1,0:T(8,128)S(1)} %get-tuple-element.22), channel_id=1, source_target_pairs={{0,8},{8,16},{16,24},{1,9},{9,17},{17,25},{2,10},{10,18},{18,26},{... | collective-permute-start | bytes 36872 | tf_op jit(solution)/shard_map/ppermute | solution.py:19
  75.7 3.8 %collective-permute-start.16 = (f32[3,1,8,128]{3,2,1,0:T(8,128)S(1)}, f32[3,1,8,128]{3,2,1,0:T(8,128)S(1)}, u32[]{:S(2)}, u32[]{:S(2)}) collective-permute-start(f32[3,1,8,128]{3,2,1,0:T(8,128)S(1)} %get-tuple-element.23), channel_id=1, source_target_pairs={{8,0},{16,8},{24,16},{9,1},{17,9},{25,17},{10,2},{18,10},{26,18},{... | collective-permute-start | bytes 36872 | tf_op jit(solution)/shard_map/ppermute | solution.py:20
  79.5 13.4 %collective-permute-start.19 = (f32[3,10,1,128]{3,2,1,0:T(1,128)S(1)}, f32[3,10,1,128]{3,2,1,0:T(1,128)S(1)}, u32[]{:S(2)}, u32[]{:S(2)}) collective-permute-start(f32[3,10,1,128]{3,2,1,0:T(1,128)S(1)} %get-tuple-element.14), channel_id=1, source_target_pairs={{0,1},{1,2},{2,3},{3,4},{4,5},{5,6},{6,7},{8,9},{9,10},{10,11},{11... | collective-permute-start | bytes 46088 | tf_op jit(solution)/shard_map/ppermute | solution.py:19
  84.3 8.6 %collective-permute-start.18 = (f32[3,10,1,128]{3,2,1,0:T(1,128)S(1)}, f32[3,10,1,128]{3,2,1,0:T(1,128)S(1)}, u32[]{:S(2)}, u32[]{:S(2)}) collective-permute-start(f32[3,10,1,128]{3,2,1,0:T(1,128)S(1)} %get-tuple-element.15), channel_id=1, source_target_pairs={{1,0},{2,1},{3,2},{4,3},{5,4},{6,5},{7,6},{9,8},{10,9},{11,10},{12... | collective-permute-start | bytes 46088 | tf_op jit(solution)/shard_map/ppermute | solution.py:20
  94.3 17.8 %copy-start.1 = (f32[3,8,8,128]{3,2,1,0:T(8,128)}, f32[3,8,8,128]{3,2,1,0:T(8,128)S(1)}, u32[]{:S(2)}) copy-start(f32[3,8,8,128]{3,2,1,0:T(8,128)S(1)} %fusion.7) | copy-start | bytes 294916
